TPU v7x, 32 devices: a whole 2x2x4 slice. The times are simulated.
32 devices in a mesh: row: 2 (over y), col: 8 (over z, core), orient: 2 (over x).
Axes of the slice: x: 2, y: 2, z: 4, core: 2. Of those that a mesh axis runs over, the one named last changes fastest.
Arguments:
- noise: float32 [2, 4096, 4096], P(None, ('row', 'col')), may hold values from -6 to 6
- elevation_library: float32 [16, 128, 128], replicated, may hold values from 0.25 to 1
- tile_choice_index: int32 [32, 32], P('row', 'col'), may hold values from 0 to 15
- family_heading_index: int32 [8], P('orient'), may hold values from 0 to 35
- family_extent_index: int32 [8], P('orient'), may hold values from 0 to 3
Outputs:
- safety_min: float32 [4096, 4096], P('row', ('col', 'orient'))
All inputs are finite; a program needn't handle non-finite values.
Results may differ from a plain program's by a relative error of at most 0.0005.
Values may be sent and summed in bfloat16 or wider, within the bound.
A program may use at most 256 MiB of HBM per device.

v0:
```python
import math
import jax
import jax.numpy as jnp
from jax import lax
from jax.sharding import PartitionSpec as P

R = 8
N_AZ = 36
NSIZE = 4
nugget_share = 0.3
peak_share = 1024.0 / (2.0 * math.pi)
cutoff_ratio = 32.0


def extended(cells, sides, width):
    for axis, dim in sides:
        count = lax.axis_size(axis)
        ends = count - 1
        head = lax.slice_in_dim(cells, 0, width, axis=dim)
        tail = lax.slice_in_dim(cells, cells.shape[dim] - width, cells.shape[dim], axis=dim)
        cells = jnp.concatenate(
            [
                lax.ppermute(tail, axis, [(i, (i + 1) % count) for i in range(ends)]),
                cells,
                lax.ppermute(head, axis, [((i + 1) % count, i) for i in range(ends)]),
            ],
            axis=dim,
        )
    return cells


def partner(x, axis, bit):
    return lax.ppermute(x, axis, [(i, i ^ 1 << bit) for i in range(lax.axis_size(axis))])


def amplitude(u_index, v_index, side_cells):
    wrap_u = jnp.minimum(u_index, side_cells - u_index).astype(jnp.float32)
    wrap_v = jnp.minimum(v_index, side_cells - v_index).astype(jnp.float32)
    cutoff = side_cells / cutoff_ratio
    scaled_u = wrap_u / cutoff
    scaled_v = wrap_v / cutoff
    grown = 1.0 + scaled_u * scaled_u + scaled_v * scaled_v
    spectrum = nugget_share + peak_share / (grown * jnp.sqrt(grown))
    return jnp.sqrt(spectrum) / side_cells


def ellipsoid(offset_u, offset_v, azimuth, size_index):
    heading = azimuth.astype(jnp.float32) * (math.pi / N_AZ)
    semi_axis = R * (size_index.astype(jnp.float32) + (1 + NSIZE)) / (2 * NSIZE)
    across = 0.6 * semi_axis
    slip_depth = 0.3 * semi_axis
    along = offset_u * jnp.cos(heading) + offset_v * jnp.sin(heading)
    lateral = offset_v * jnp.cos(heading) - offset_u * jnp.sin(heading)
    along_part = along / semi_axis
    lateral_part = lateral / across
    inside = 1.0 - along_part * along_part - lateral_part * lateral_part
    height = slip_depth * jnp.sqrt(jnp.maximum(inside, 0.0))
    base_share = jnp.clip(4.0 * inside, 0.0, 1.0)
    return (height, base_share)


def angle_table(row_count, col_count, period):
    left_index = lax.broadcasted_iota(jnp.int32, (row_count, col_count), 0)
    right_index = lax.broadcasted_iota(jnp.int32, (row_count, col_count), 1)
    phase_step = left_index * right_index % period
    angles = phase_step.astype(jnp.float32) * (2.0 * math.pi / period)
    return (jnp.cos(angles), jnp.sin(angles))


def transform_last(real_part, imag_part):
    length = real_part.shape[-1]
    inner_size = 128
    outer_size = length // inner_size
    leading = real_part.shape[:-1]
    real_in = real_part.reshape(leading + (outer_size, inner_size))
    imag_in = imag_part.reshape(leading + (outer_size, inner_size))
    highest = lax.Precision.HIGHEST
    outer_cos, outer_sin = angle_table(outer_size, outer_size, outer_size)
    real_mid = jnp.einsum("...pq,pk->...kq", real_in, outer_cos, precision=highest) + jnp.einsum(
        "...pq,pk->...kq", imag_in, outer_sin, precision=highest
    )
    imag_mid = jnp.einsum("...pq,pk->...kq", imag_in, outer_cos, precision=highest) - jnp.einsum(
        "...pq,pk->...kq", real_in, outer_sin, precision=highest
    )
    twist_cos, twist_sin = angle_table(outer_size, inner_size, length)
    real_twist = real_mid * twist_cos + imag_mid * twist_sin
    imag_twist = imag_mid * twist_cos - real_mid * twist_sin
    inner_cos, inner_sin = angle_table(inner_size, inner_size, inner_size)
    real_out = jnp.einsum("...kq,ql->...kl", real_twist, inner_cos, precision=highest) + jnp.einsum(
        "...kq,ql->...kl", imag_twist, inner_sin, precision=highest
    )
    imag_out = jnp.einsum("...kq,ql->...kl", imag_twist, inner_cos, precision=highest) - jnp.einsum(
        "...kq,ql->...kl", real_twist, inner_sin, precision=highest
    )
    real_out = jnp.swapaxes(real_out, -1, -2).reshape(leading + (length,))
    imag_out = jnp.swapaxes(imag_out, -1, -2).reshape(leading + (length,))
    return (real_out, imag_out)


def body(noise, elevation_library, tile_choice_index, family_heading_index, family_extent_index):
    line_count = noise.shape[1]
    side_cells = noise.shape[2]
    first_line = lax.axis_index(("row", "col")) * line_count
    v_index = first_line + lax.broadcasted_iota(jnp.int32, (line_count, side_cells), 0)
    u_index = lax.broadcasted_iota(jnp.int32, (line_count, side_cells), 1)
    amplitudes = amplitude(u_index, v_index, side_cells)
    real_part, imag_part = transform_last(noise[0] * amplitudes, noise[1] * amplitudes)
    spectrum = jnp.stack([real_part, imag_part])
    transposed = lax.all_to_all(
        spectrum.astype(jnp.bfloat16), ("row", "col"), split_axis=2, concat_axis=1, tiled=True
    ).astype(spectrum.dtype)
    turned = jnp.swapaxes(transposed, 1, 2)
    field_re, field_im = transform_last(turned[0], turned[1])
    fields = lax.all_to_all(
        jnp.stack([field_re, field_im]).astype(jnp.bfloat16),
        "col",
        split_axis=2,
        concat_axis=1,
        tiled=True,
    ).astype(jnp.float32)
    window_rows = fields.shape[1]
    window_columns = fields.shape[2]
    elevation_tiles = jnp.take(elevation_library, tile_choice_index, axis=0)
    slope_tangents = elevation_tiles.transpose(0, 2, 1, 3).reshape(window_rows, window_columns)
    secant = jnp.sqrt(1.0 + slope_tangents * slope_tangents)
    cohesion = 0.5 * jnp.exp(0.4 * fields[0])
    friction = 0.6 * jnp.exp(0.25 * fields[1])
    column_terms = jnp.stack(
        [cohesion * secant, friction / secant, slope_tangents / secant]
    ).astype(jnp.bfloat16)
    padded = extended(column_terms, (("row", 1), ("col", 2)), R)
    tile_width = min(128, window_columns)
    tile_count = window_columns // tile_width
    strip_span = tile_width + 2 * R
    strips = jnp.stack(
        [
            padded[:, :, tile_index * tile_width : tile_index * tile_width + strip_span]
            for tile_index in range(tile_count)
        ],
        axis=2,
    )
    kernel_width = 2 * R + 1
    shift_index = lax.broadcasted_iota(jnp.int32, (kernel_width, strip_span, tile_width), 0)
    strip_index = lax.broadcasted_iota(jnp.int32, (kernel_width, strip_span, tile_width), 1)
    out_index = lax.broadcasted_iota(jnp.int32, (kernel_width, strip_span, tile_width), 2)
    column_gap = strip_index - out_index
    offset_u = (shift_index - R).astype(jnp.float32)
    offset_v = (column_gap - R).astype(jnp.float32)
    inside_band = (column_gap >= 0) & (column_gap <= 2 * R)
    height, base_share = ellipsoid(
        offset_u[None],
        offset_v[None],
        family_heading_index[:, None, None, None],
        family_extent_index[:, None, None, None],
    )
    band_height = jnp.where(inside_band[None], height, 0.0).astype(jnp.bfloat16)
    band_share = jnp.where(inside_band[None], base_share, 0.0).astype(jnp.bfloat16)
    shifted = jnp.stack(
        [strips[:, row_shift : row_shift + window_rows] for row_shift in range(kernel_width)],
        axis=1,
    )
    resist_kernel = jnp.stack([band_share, band_height])
    resisting = jnp.einsum(
        "csxti,cfsio->fxto", shifted[0:2], resist_kernel, preferred_element_type=jnp.float32
    )
    driving = jnp.einsum(
        "sxti,fsio->fxto", shifted[2], band_height, preferred_element_type=jnp.float32
    )
    safety = resisting / driving
    family_low = jnp.min(safety, axis=0).reshape(window_rows, window_columns)
    half_width = window_columns // 2
    side_index = lax.axis_index("orient")
    own_half = lax.dynamic_slice_in_dim(family_low, side_index * half_width, half_width, 1)
    other_half = lax.dynamic_slice_in_dim(family_low, (1 - side_index) * half_width, half_width, 1)
    partner_half = partner(other_half, "orient", 0)
    return jnp.minimum(own_half, partner_half)


def solution(mesh):
    placed = (P(None, ("row", "col"), None), P(), P("row", "col"), P("orient"), P("orient"))
    return jax.shard_map(
        body, mesh=mesh, in_specs=placed, out_specs=P("row", ("col", "orient")), check_vma=False
    )
```

profile of v0, /device:TPU:0, one launch (start us, length us, event | category | flops | bytes accessed | tf_op | source)
XLA Modules:
  0.0 706.0 jit_solution(4212948183642729390)
XLA Ops:
  27.4 6.4 fusion.42
  33.8 7.0 fusion.40
  40.8 6.5 fusion.60
  48.7 6.8 fusion.61
  57.0 25.5 %copy.105 = bf16[2,256,4096]{1,0,2:T(2,128)(2,1)S(1)} copy(bf16[2,256,4096]{1,2,0:T(8,128)(2,1)S(1)} %pad_maximum_fusion.2) | data formatting | bytes 8388608 | tf_op jit(solution)/shard_map/stack | solution.py:108
  82.5 99.9 %all_to_all.27 = bf16[2,256,4096]{1,0,2:T(2,128)(2,1)S(1)} all-to-all(bf16[2,256,4096]{1,0,2:T(2,128)(2,1)S(1)} %copy.105), channel_id=1, replica_groups=mesh['row'=2,'col'=8,'orient'=2] {'row','col'}, dimensions={2} | all-to-all | bytes 8388608 | tf_op jit(solution)/shard_map/all_to_all | solution.py:109
  216.7 6.8 fusion.34
  223.5 6.8 fusion.32
  230.3 7.2 %fusion.62 = bf16[256,128,32]{0,1,2:T(8,128)(2,1)S(1)} fusion(f32[256,32,128]{0,2,1:T(8,128)S(1)} %fusion.34, f32[256,32,128]{2,1,0:T(8,128)S(1)} %get-tuple-element.5), kind=kOutput, calls=%fused_computation.116 | convolution fusion | flops 1612939264 | bytes 10485760 | tf_op jit(solution)/shard_map/...kq,ql->...kl/dot_general | solution.py:89
  238.7 6.7 fusion.63
  247.0 27.2 %copy.116 = bf16[2,256,4096]{1,0,2:T(2,128)(2,1)} copy(bf16[2,256,4096]{1,2,0:T(8,128)(2,1)S(1)} %pad_maximum_fusion.3) | data formatting | bytes 8388608 | tf_op jit(solution)/shard_map/stack | solution.py:115
  298.7 74.4 %all-to-all-done.1 = bf16[2,256,4096]{1,0,2:T(2,128)(2,1)} async-done(((bf16[2,256,4096]{1,0,2:T(2,128)(2,1)}), bf16[2,256,4096]{1,0,2:T(2,128)(2,1)}, u32[]{:S(2)}, u32[]{:S(2)}) %all-to-all-start.1) | async-done | bytes 4194336 | tf_op jit(solution)/shard_map/all_to_all | solution.py:114
  412.2 12.7 %concatenate.10 = bf16[3,2064,512]{1,2,0:T(8,128)(2,1)} concatenate(bf16[3,8,512]{1,2,0:T(8,128)(2,1)} %copy-done.11, bf16[3,2048,512]{1,2,0:T(8,128)(2,1)} %copy-done.2, bf16[3,8,512]{1,2,0:T(8,128)(2,1)} %collective-permute-done.1), dimensions={1} | concatenate | bytes 12681216 | tf_op jit(solution)/shard_map/concatenate | solution.py:21
  444.1 6.7 fusion.18
  450.9 6.7 fusion.17
  457.6 6.7 fusion.16
  464.2 6.9 fusion.15
  471.1 6.7 fusion.14
  477.8 6.7 fusion.13
  484.5 6.9 fusion.12
  491.4 6.7 fusion.11
  498.1 6.7 fusion.10
  504.8 7.0 fusion.9
  511.9 6.7 fusion.8
  518.6 6.6 fusion.7
  525.2 6.8 fusion.6
  532.1 6.7 fusion.5
  538.8 6.7 fusion.4
  545.5 6.6 fusion.3
  552.2 51.8 %fusion = f32[4,128,2048,4,1,1]{2,1,5,4,3,0:T(8,128)} fusion(bf16[3,17,2048,4,144]{2,4,1,0,3:T(8,128)(2,1)} %fusion.3, bf16[2,4,17,144,128,1]{4,3,2,0,5,1:T(8,128)(2,1)} %maximum_bitcast_fusion.4), kind=kOutput, calls=%fused_computation.2 | convolution fusion | flops 41070624768 | bytes 102006784 | tf_op jit(solution)/shard_map/csxti,cfsio->fxto/dot_general | solution.py:163
  604.1 42.4 %fusion.2 = f32[128,2048,4]{1,0,2:T(8,128)} fusion(f32[4,128,2048,4,1,1]{2,1,5,4,3,0:T(8,128)} %fusion, bf16[3,17,2048,4,144]{2,4,1,0,3:T(8,128)(2,1)} %fusion.3, f32[4]{0:T(128)S(1)} %copy-done.16, f32[4]{0:T(128)S(1)} %copy-done.14, f32[4]{0:T(128)S(1)} %copy-done.20, f32[17,144,128]{2,1,0:T(8,128)S(1)} %copy-done.8, f32[4]{0:T(128)S(1)} %copy-done.22, ...), kind=kOutput, calls=%fused_computation.6 | convolution fusion | flops 20562706432 | bytes 62646420 | tf_op jit(solution)/shard_map/sxti,fsio->fxto/dot_general | solution.py:166
  656.6 45.4 %collective-permute-done.4 = f32[2048,256]{1,0:T(8,128)} collective-permute-done((f32[2048,256]{1,0:T(8,128)}, f32[2048,256]{1,0:T(8,128)}, u32[]{:S(2)}, u32[]{:S(2)}) %collective-permute-start.4) | collective-permute-done | bytes 2097184 | tf_op jit(solution)/shard_map/ppermute | solution.py:33
  (121 shorter events, 163.6 us)
Async XLA Ops:
  0.0 279.3 %copy-start = (f32[16,128,128]{2,1,0:T(8,128)S(1)}, f32[16,128,128]{2,1,0:T(8,128)}, u32[]{:S(2)}) copy-start(f32[16,128,128]{2,1,0:T(8,128)} %param.6) | copy-start | bytes 3145732
  207.9 3.8 copy-start.3
  207.9 3.8 copy-start.4
  274.2 4.9 copy-start.12
  274.2 98.9 %all-to-all-start.1 = ((bf16[2,256,4096]{1,0,2:T(2,128)(2,1)}), bf16[2,256,4096]{1,0,2:T(2,128)(2,1)}, u32[]{:S(2)}, u32[]{:S(2)}) async-start(bf16[2,256,4096]{1,0,2:T(2,128)(2,1)} %copy.116), calls=%async_computation.1 | async-start | bytes 8388608 | tf_op jit(solution)/shard_map/all_to_all | solution.py:114
  292.2 6.3 copy-start.25
  292.2 6.3 copy-start.26
  297.2 103.9 %copy-start.23 = (f32[17]{0:T(128)}, f32[17]{0:T(128)S(1)}, u32[]{:S(2)}) copy-start(f32[17]{0:T(128)S(1)} %add_convert_fusion.3) | copy-start | bytes 208
  297.3 103.8 %copy-start.9 = (pred[17,144,128]{2,1,0:T(8,128)(4,1)}, pred[17,144,128]{2,1,0:T(8,128)(4,1)S(1)}, u32[]{:S(2)}) copy-start(pred[17,144,128]{2,1,0:T(8,128)(4,1)S(1)} %fusion.76) | copy-start | bytes 940036
  298.6 102.5 %copy-start.13 = (f32[4]{0:T(128)}, f32[4]{0:T(128)S(1)}, u32[]{:S(2)}) copy-start(f32[4]{0:T(128)S(1)} %get-tuple-element.34) | copy-start | bytes 52
  298.6 102.5 %copy-start.15 = (f32[4]{0:T(128)}, f32[4]{0:T(128)S(1)}, u32[]{:S(2)}) copy-start(f32[4]{0:T(128)S(1)} %get-tuple-element.35) | copy-start | bytes 52
  298.6 102.5 %copy-start.17 = (f32[4]{0:T(128)}, f32[4]{0:T(128)S(1)}, u32[]{:S(2)}) copy-start(f32[4]{0:T(128)S(1)} %get-tuple-element.36) | copy-start | bytes 52
  298.6 102.5 %copy-start.19 = (f32[4]{0:T(128)}, f32[4]{0:T(128)S(1)}, u32[]{:S(2)}) copy-start(f32[4]{0:T(128)S(1)} %get-tuple-element.39) | copy-start | bytes 52
  298.6 102.5 %copy-start.21 = (f32[4]{0:T(128)}, f32[4]{0:T(128)S(1)}, u32[]{:S(2)}) copy-start(f32[4]{0:T(128)S(1)} %get-tuple-element.40) | copy-start | bytes 52
  380.0 2.2 copy-start.6
  382.2 2.2 copy-start.5
  389.7 11.5 %copy-start.7 = (f32[17,144,128]{2,1,0:T(8,128)S(1)}, f32[17,144,128]{2,1,0:T(8,128)}, u32[]{:S(2)}) copy-start(f32[17,144,128]{2,1,0:T(8,128)} %add_convert_fusion.2) | copy-start | bytes 3760132
  393.5 2.7 copy-start.2
  396.4 11.5 %collective-permute-start = (bf16[3,8,512]{1,2,0:T(8,128)(2,1)S(1)}, bf16[3,8,512]{1,2,0:T(8,128)(2,1)S(1)}, u32[]{:S(2)}, u32[]{:S(2)}) collective-permute-start(bf16[3,8,512]{1,2,0:T(8,128)(2,1)S(1)} %get-tuple-element.20), channel_id=1, source_target_pairs={{0,16},{1,17},{2,18},{3,19},{4,20},{5,21},{6,22},{7,23},{8,24},{9,... | collective-permute-start | bytes 73736 | tf_op jit(solution)/shard_map/ppermute | solution.py:23
  399.8 12.4 %collective-permute-start.1 = (bf16[3,8,512]{1,2,0:T(8,128)(2,1)S(1)}, bf16[3,8,512]{1,2,0:T(8,128)(2,1)}, u32[]{:S(2)}, u32[]{:S(2)}) collective-permute-start(bf16[3,8,512]{1,2,0:T(8,128)(2,1)S(1)} %get-tuple-element.19), channel_id=1, source_target_pairs={{16,0},{17,1},{18,2},{19,3},{20,4},{21,5},{22,6},{23,7},{24,8},{25... | collective-permute-start | bytes 73736 | tf_op jit(solution)/shard_map/ppermute | solution.py:25
  425.9 7.0 collective-permute-start.2
  427.2 5.7 collective-permute-start.3
  552.2 51.9 %copy-start.8 = (f32[17,144,128]{2,1,0:T(8,128)S(1)}, f32[17,144,128]{2,1,0:T(8,128)}, u32[]{:S(2)}) copy-start(f32[17,144,128]{2,1,0:T(8,128)} %add_convert_fusion.2) | copy-start | bytes 3760132
  552.2 51.9 %copy-start.10 = (pred[17,144,128]{2,1,0:T(8,128)(4,1)S(1)}, pred[17,144,128]{2,1,0:T(8,128)(4,1)}, u32[]{:S(2)}) copy-start(pred[17,144,128]{2,1,0:T(8,128)(4,1)} %copy-done.9) | copy-start | bytes 940036
  552.2 51.9 %copy-start.14 = (f32[4]{0:T(128)S(1)}, f32[4]{0:T(128)}, u32[]{:S(2)}) copy-start(f32[4]{0:T(128)} %copy-done.13) | copy-start | bytes 52
  552.2 51.9 %copy-start.16 = (f32[4]{0:T(128)S(1)}, f32[4]{0:T(128)}, u32[]{:S(2)}) copy-start(f32[4]{0:T(128)} %copy-done.15) | copy-start | bytes 52
  552.2 51.9 %copy-start.18 = (f32[4]{0:T(128)S(1)}, f32[4]{0:T(128)}, u32[]{:S(2)}) copy-start(f32[4]{0:T(128)} %copy-done.17) | copy-start | bytes 52
  552.2 51.9 %copy-start.20 = (f32[4]{0:T(128)S(1)}, f32[4]{0:T(128)}, u32[]{:S(2)}) copy-start(f32[4]{0:T(128)} %copy-done.19) | copy-start | bytes 52
  552.2 51.9 %copy-start.22 = (f32[4]{0:T(128)S(1)}, f32[4]{0:T(128)}, u32[]{:S(2)}) copy-start(f32[4]{0:T(128)} %copy-done.21) | copy-start | bytes 52
  552.2 51.9 %copy-start.24 = (f32[17]{0:T(128)S(1)}, f32[17]{0:T(128)}, u32[]{:S(2)}) copy-start(f32[17]{0:T(128)} %copy-done.23) | copy-start | bytes 208
  653.3 48.7 %collective-permute-start.4 = (f32[2048,256]{1,0:T(8,128)}, f32[2048,256]{1,0:T(8,128)}, u32[]{:S(2)}, u32[]{:S(2)}) collective-permute-start(f32[2048,256]{1,0:T(8,128)} %copy.147), channel_id=1, source_target_pairs={{0,1},{1,0},{2,3},{3,2},{4,5},{5,4},{6,7},{7,6},{8,9},{9,8},{10,11... | collective-permute-start | bytes 6291464 | tf_op jit(solution)/shard_map/ppermute | solution.py:33
  654.8 51.0 %copy-start.1 = (f32[16,128,128]{2,1,0:T(8,128)S(1)}, f32[16,128,128]{2,1,0:T(8,128)}, u32[]{:S(2)}) copy-start(f32[16,128,128]{2,1,0:T(8,128)} %param.6) | copy-start | bytes 3145732
  (1 other events, 0.7 us)
where the time goes:
time: 711 us; the launch traced here: 706 us
  local copies, waits for them, and re-layouts  243 us (34%)
  matrix products  178 us (25%)
  waiting for transfers between devices  125 us (18%)
  blocking collectives  99.9 us (14%)
  other arithmetic  45.5 us (6%)
  starting transfers between devices  13.6 us (2%)
    unnamed x75, local copies, waits for them, and re-layouts  122 us
    all_to_all x1, blocking collectives, body(): lax.all_to_all(spectrum.astype(jnp.bfloat16), ('row', 'col'), split_axis=...  99.9 us
    all_to_all x1, waiting for transfers between devices, body(): lax.all_to_all(jnp.stack([field_re, field_im]).astype(jnp.bfloat16), 'col...  74.4 us
    dot_general x1, matrix products, body(): jnp.einsum('csxti,cfsio->fxto', shifted[0:2], resist_kernel, preferred_el...  51.8 us
    ppermute x1, waiting for transfers between devices, partner(): lax.ppermute(x, axis, [(i, i ^ 1 << bit) for i in range(lax.axis_size(axi...  45.4 us
    dot_general x1, matrix products, body(): jnp.einsum('sxti,fsio->fxto', shifted[2], band_height, preferred_element_...  42.4 us
    another operation x1, local copies, waits for them, and re-layouts, body(): jnp.stack([field_re, field_im]).astype(jnp.bfloat16)  27.2 us
    another operation x1, local copies, waits for them, and re-layouts, body(): spectrum = jnp.stack([real_part, imag_part])  25.5 us
  transfers between devices with their start and end apart: 6, of which 4 were waited for; matrix products, arithmetic and copies ran while one was open for 4% of the time, Pallas kernels for 0%

commit v1 on v0

--- a/solution.py
+++ b/solution.py
@@ -106,8 +106,16 @@
     amplitudes = amplitude(u_index, v_index, side_cells)
     real_part, imag_part = transform_last(noise[0] * amplitudes, noise[1] * amplitudes)
     spectrum = jnp.stack([real_part, imag_part])
-    transposed = lax.all_to_all(
-        spectrum.astype(jnp.bfloat16), ("row", "col"), split_axis=2, concat_axis=1, tiled=True
+    transposed = jnp.concatenate(
+        lax.all_to_all(
+            jnp.stack(
+                jnp.split(spectrum.astype(jnp.bfloat16), lax.axis_size(("row", "col")), axis=2)
+            ),
+            ("row", "col"),
+            0,
+            0,
+        ),
+        axis=1,
     ).astype(spectrum.dtype)
     turned = jnp.swapaxes(transposed, 1, 2)
     field_re, field_im = transform_last(turned[0], turned[1])

time: 711 us -> 683 us (0.961)
  local copies, waits for them, and re-layouts: 243 us -> 215 us
    another operation x1 -> x0, local copies, waits for them, and re-layouts: 25.5 us -> none  [body(): spectrum = jnp.stack([real_part, imag_part])]
    all_to_all x2 -> x0, local copies, waits for them, and re-layouts: 8.77 us -> none  [body(): lax.all_to_all(spectrum.astype(jnp.bfloat16), ('row', 'col'), split_axis=...]
  transfers between devices with their start and end apart: 6 -> 6, of which waited for: 4 -> 4; matrix products, arithmetic and copies ran while one was open for 4% -> 5% of each run, Pallas kernels for 0% -> 0%
where the time goes in v1:
time: 683 us; the launch traced here: 678 us
  local copies, waits for them, and re-layouts  215 us (31%)
  matrix products  178 us (26%)
  waiting for transfers between devices  125 us (18%)
  blocking collectives  100 us (15%)
  other arithmetic  45.4 us (7%)
  starting transfers between devices  13.6 us (2%)
    unnamed x75, local copies, waits for them, and re-layouts  122 us
    all_to_all x1, blocking collectives, body(): lax.all_to_all(jnp.stack(jnp.split(spectrum.astype(jnp.bfloat16), lax.axi...  100 us
    all_to_all x1, waiting for transfers between devices, body(): lax.all_to_all(jnp.stack([field_re, field_im]).astype(jnp.bfloat16), 'col...  74.4 us
    dot_general x1, matrix products, body(): jnp.einsum('csxti,cfsio->fxto', shifted[0:2], resist_kernel, preferred_el...  51.8 us
    ppermute x1, waiting for transfers between devices, partner(): lax.ppermute(x, axis, [(i, i ^ 1 << bit) for i in range(lax.axis_size(axi...  45.4 us
    dot_general x1, matrix products, body(): jnp.einsum('sxti,fsio->fxto', shifted[2], band_height, preferred_element_...  42.4 us
    another operation x1, local copies, waits for them, and re-layouts, body(): jnp.stack([field_re, field_im]).astype(jnp.bfloat16)  27.2 us
    dot_general x2, matrix products, transform_last(): jnp.einsum('...kq,ql->...kl', imag_twist, inner_cos, precision=highest)  13.8 us
  transfers between devices with their start and end apart: 6, of which 4 were waited for; matrix products, arithmetic and copies ran while one was open for 5% of the time, Pallas kernels for 0%

profile of v1, /device:TPU:0, one launch (start us, length us, event | category | flops | bytes accessed | tf_op | source)
XLA Modules:
  0.0 678.2 jit_solution(12159289963111398564)
XLA Ops:
  27.4 6.4 fusion.42
  33.8 7.0 %fusion.40 = f32[256,32,128]{0,2,1:T(8,128)S(1)} fusion(f32[256,32,128]{2,1,0:T(8,128)S(1)} %get-tuple-element.8), kind=kOutput, calls=%fused_computation.120 | convolution fusion | flops 1610842112 | bytes 8388608 | tf_op jit(solution)/shard_map/...kq,ql->...kl/dot_general | solution.py:92
  40.8 6.5 fusion.60
  48.7 6.8 fusion.61
  57.1 100.0 %all_to_all.14 = bf16[16,2,256,256]{2,3,1,0:T(8,128)(2,1)} all-to-all(bf16[16,2,256,256]{2,3,1,0:T(8,128)(2,1)S(1)} %fusion.93), channel_id=1, replica_groups=mesh['row'=2,'col'=8,'orient'=2] {'row','col'}, dimensions={0} | all-to-all | bytes 8388608 | tf_op jit(solution)/shard_map/all_to_all | solution.py:110
  157.1 6.2 copy.126
  188.8 6.8 %fusion.34 = f32[256,32,128]{0,2,1:T(8,128)S(1)} fusion(f32[256,32,128]{2,1,0:T(8,128)S(1)} %get-tuple-element.6), kind=kOutput, calls=%fused_computation.114 | convolution fusion | flops 1610842112 | bytes 8388608 | tf_op jit(solution)/shard_map/...kq,ql->...kl/dot_general | solution.py:89
  195.6 6.8 fusion.32
  202.4 7.2 %fusion.62 = bf16[256,128,32]{0,1,2:T(8,128)(2,1)S(1)} fusion(f32[256,32,128]{0,2,1:T(8,128)S(1)} %fusion.34, f32[256,32,128]{2,1,0:T(8,128)S(1)} %get-tuple-element.5), kind=kOutput, calls=%fused_computation.145 | convolution fusion | flops 1612939264 | bytes 10485760 | tf_op jit(solution)/shard_map/...kq,ql->...kl/dot_general | solution.py:89
  210.8 6.7 fusion.63
  219.1 27.2 %copy.135 = bf16[2,256,4096]{1,0,2:T(2,128)(2,1)} copy(bf16[2,256,4096]{1,2,0:T(8,128)(2,1)S(1)} %pad_maximum_fusion.2) | data formatting | bytes 8388608 | tf_op jit(solution)/shard_map/stack | solution.py:123
  270.8 74.4 %all-to-all-done.1 = bf16[2,256,4096]{1,0,2:T(2,128)(2,1)} async-done(((bf16[2,256,4096]{1,0,2:T(2,128)(2,1)}), bf16[2,256,4096]{1,0,2:T(2,128)(2,1)}, u32[]{:S(2)}, u32[]{:S(2)}) %all-to-all-start.1) | async-done | bytes 4194336 | tf_op jit(solution)/shard_map/all_to_all | solution.py:122
  384.3 12.7 %concatenate.10 = bf16[3,2064,512]{1,2,0:T(8,128)(2,1)} concatenate(bf16[3,8,512]{1,2,0:T(8,128)(2,1)} %copy-done.11, bf16[3,2048,512]{1,2,0:T(8,128)(2,1)} %copy-done.2, bf16[3,8,512]{1,2,0:T(8,128)(2,1)} %collective-permute-done.1), dimensions={1} | concatenate | bytes 12681216 | tf_op jit(solution)/shard_map/concatenate | solution.py:21
  416.3 6.7 fusion.18
  423.0 6.7 fusion.17
  429.7 6.7 fusion.16
  436.4 6.9 %fusion.15 = bf16[3,17,2048,4,144]{2,4,1,0,3:T(8,128)(2,1)} fusion(bf16[3,17,2048,4,144]{2,4,1,0,3:T(8,128)(2,1)} %fusion.16, bf16[3,2064,4,144]{1,3,0,2:T(8,128)(2,1)S(1)} %pad_maximum_fusion), kind=kLoop, calls=%fused_computation.64 | loop fusion | bytes 14155776
  443.2 6.7 fusion.14
  450.0 6.7 fusion.13
  456.7 6.9 %fusion.12 = bf16[3,17,2048,4,144]{2,4,1,0,3:T(8,128)(2,1)} fusion(bf16[3,17,2048,4,144]{2,4,1,0,3:T(8,128)(2,1)} %fusion.13, bf16[3,2064,4,144]{1,3,0,2:T(8,128)(2,1)S(1)} %pad_maximum_fusion), kind=kLoop, calls=%fused_computation.58 | loop fusion | bytes 14155776
  463.6 6.7 fusion.11
  470.2 6.7 fusion.10
  477.0 7.0 %fusion.9 = bf16[3,17,2048,4,144]{2,4,1,0,3:T(8,128)(2,1)} fusion(bf16[3,17,2048,4,144]{2,4,1,0,3:T(8,128)(2,1)} %fusion.10, bf16[3,2064,4,144]{1,3,0,2:T(8,128)(2,1)S(1)} %pad_maximum_fusion), kind=kLoop, calls=%fused_computation.52 | loop fusion | bytes 14155776
  484.0 6.7 fusion.8
  490.7 6.6 fusion.7
  497.4 6.8 %fusion.6 = bf16[3,17,2048,4,144]{2,4,1,0,3:T(8,128)(2,1)} fusion(bf16[3,17,2048,4,144]{2,4,1,0,3:T(8,128)(2,1)} %fusion.7, bf16[3,2064,4,144]{1,3,0,2:T(8,128)(2,1)S(1)} %pad_maximum_fusion), kind=kLoop, calls=%fused_computation.46 | loop fusion | bytes 14155776
  504.2 6.7 fusion.5
  510.9 6.7 fusion.4
  517.7 6.6 fusion.3
  524.4 51.8 %fusion = f32[4,128,2048,4,1,1]{2,1,5,4,3,0:T(8,128)} fusion(bf16[3,17,2048,4,144]{2,4,1,0,3:T(8,128)(2,1)} %fusion.3, bf16[2,4,17,144,128,1]{4,3,2,0,5,1:T(8,128)(2,1)} %maximum_bitcast_fusion.4), kind=kOutput, calls=%fused_computation.2 | convolution fusion | flops 41070624768 | bytes 102006784 | tf_op jit(solution)/shard_map/csxti,cfsio->fxto/dot_general | solution.py:171
  576.2 42.4 %fusion.2 = f32[128,2048,4]{1,0,2:T(8,128)} fusion(f32[4,128,2048,4,1,1]{2,1,5,4,3,0:T(8,128)} %fusion, bf16[3,17,2048,4,144]{2,4,1,0,3:T(8,128)(2,1)} %fusion.3, f32[4]{0:T(128)S(1)} %copy-done.16, f32[4]{0:T(128)S(1)} %copy-done.14, f32[4]{0:T(128)S(1)} %copy-done.20, f32[17,144,128]{2,1,0:T(8,128)S(1)} %copy-done.8, f32[4]{0:T(128)S(1)} %copy-done.22, ...), kind=kOutput, calls=%fused_computation.6 | convolution fusion | flops 20562706432 | bytes 62646420 | tf_op jit(solution)/shard_map/sxti,fsio->fxto/dot_general | solution.py:174
  628.8 45.4 %collective-permute-done.4 = f32[2048,256]{1,0:T(8,128)} collective-permute-done((f32[2048,256]{1,0:T(8,128)}, f32[2048,256]{1,0:T(8,128)}, u32[]{:S(2)}, u32[]{:S(2)}) %collective-permute-start.4) | collective-permute-done | bytes 2097184 | tf_op jit(solution)/shard_map/ppermute | solution.py:33
  (134 shorter events, 154.8 us)
Async XLA Ops:
  0.0 251.4 %copy-start = (f32[16,128,128]{2,1,0:T(8,128)S(1)}, f32[16,128,128]{2,1,0:T(8,128)}, u32[]{:S(2)}) copy-start(f32[16,128,128]{2,1,0:T(8,128)} %param.6) | copy-start | bytes 3145732
  180.0 3.8 copy-start.3
  180.0 3.8 copy-start.4
  246.4 4.9 copy-start.12
  246.4 98.9 %all-to-all-start.1 = ((bf16[2,256,4096]{1,0,2:T(2,128)(2,1)}), bf16[2,256,4096]{1,0,2:T(2,128)(2,1)}, u32[]{:S(2)}, u32[]{:S(2)}) async-start(bf16[2,256,4096]{1,0,2:T(2,128)(2,1)} %copy.135), calls=%async_computation.1 | async-start | bytes 8388608 | tf_op jit(solution)/shard_map/all_to_all | solution.py:122
  264.3 6.3 copy-start.25
  264.3 6.3 copy-start.26
  269.3 103.9 %copy-start.23 = (f32[17]{0:T(128)}, f32[17]{0:T(128)S(1)}, u32[]{:S(2)}) copy-start(f32[17]{0:T(128)S(1)} %add_convert_fusion.3) | copy-start | bytes 208
  269.4 103.8 %copy-start.9 = (pred[17,144,128]{2,1,0:T(8,128)(4,1)}, pred[17,144,128]{2,1,0:T(8,128)(4,1)S(1)}, u32[]{:S(2)}) copy-start(pred[17,144,128]{2,1,0:T(8,128)(4,1)S(1)} %fusion.76) | copy-start | bytes 940036
  270.7 102.6 %copy-start.13 = (f32[4]{0:T(128)}, f32[4]{0:T(128)S(1)}, u32[]{:S(2)}) copy-start(f32[4]{0:T(128)S(1)} %get-tuple-element.34) | copy-start | bytes 52
  270.7 102.6 %copy-start.15 = (f32[4]{0:T(128)}, f32[4]{0:T(128)S(1)}, u32[]{:S(2)}) copy-start(f32[4]{0:T(128)S(1)} %get-tuple-element.35) | copy-start | bytes 52
  270.7 102.6 %copy-start.17 = (f32[4]{0:T(128)}, f32[4]{0:T(128)S(1)}, u32[]{:S(2)}) copy-start(f32[4]{0:T(128)S(1)} %get-tuple-element.36) | copy-start | bytes 52
  270.7 102.6 %copy-start.19 = (f32[4]{0:T(128)}, f32[4]{0:T(128)S(1)}, u32[]{:S(2)}) copy-start(f32[4]{0:T(128)S(1)} %get-tuple-element.39) | copy-start | bytes 52
  270.8 102.6 %copy-start.21 = (f32[4]{0:T(128)}, f32[4]{0:T(128)S(1)}, u32[]{:S(2)}) copy-start(f32[4]{0:T(128)S(1)} %get-tuple-element.40) | copy-start | bytes 52
  352.1 2.2 copy-start.6
  354.3 2.2 copy-start.5
  361.8 11.5 %copy-start.7 = (f32[17,144,128]{2,1,0:T(8,128)S(1)}, f32[17,144,128]{2,1,0:T(8,128)}, u32[]{:S(2)}) copy-start(f32[17,144,128]{2,1,0:T(8,128)} %add_convert_fusion.2) | copy-start | bytes 3760132
  365.6 2.7 copy-start.2
  368.5 11.6 %collective-permute-start = (bf16[3,8,512]{1,2,0:T(8,128)(2,1)S(1)}, bf16[3,8,512]{1,2,0:T(8,128)(2,1)S(1)}, u32[]{:S(2)}, u32[]{:S(2)}) collective-permute-start(bf16[3,8,512]{1,2,0:T(8,128)(2,1)S(1)} %get-tuple-element.20), channel_id=1, source_target_pairs={{0,16},{1,17},{2,18},{3,19},{4,20},{5,21},{6,22},{7,23},{8,24},{9,... | collective-permute-start | bytes 73736 | tf_op jit(solution)/shard_map/ppermute | solution.py:23
  371.9 12.4 %collective-permute-start.1 = (bf16[3,8,512]{1,2,0:T(8,128)(2,1)S(1)}, bf16[3,8,512]{1,2,0:T(8,128)(2,1)}, u32[]{:S(2)}, u32[]{:S(2)}) collective-permute-start(bf16[3,8,512]{1,2,0:T(8,128)(2,1)S(1)} %get-tuple-element.19), channel_id=1, source_target_pairs={{16,0},{17,1},{18,2},{19,3},{20,4},{21,5},{22,6},{23,7},{24,8},{25... | collective-permute-start | bytes 73736 | tf_op jit(solution)/shard_map/ppermute | solution.py:25
  398.0 7.0 %collective-permute-start.2 = (bf16[3,2064,8]{1,2,0:T(8,128)(2,1)S(1)}, bf16[3,2064,8]{1,2,0:T(8,128)(2,1)S(1)}, u32[]{:S(2)}, u32[]{:S(2)}) collective-permute-start(bf16[3,2064,8]{1,2,0:T(8,128)(2,1)S(1)} %get-tuple-element.17), channel_id=1, source_target_pairs={{0,2},{2,4},{4,6},{6,8},{8,10},{10,12},{12,14},{1,3},{3,5},{5,7},{... | collective-permute-start | bytes 297224 | tf_op jit(solution)/shard_map/ppermute | solution.py:23
  399.3 5.7 collective-permute-start.3
  524.3 51.9 %copy-start.8 = (f32[17,144,128]{2,1,0:T(8,128)S(1)}, f32[17,144,128]{2,1,0:T(8,128)}, u32[]{:S(2)}) copy-start(f32[17,144,128]{2,1,0:T(8,128)} %add_convert_fusion.2) | copy-start | bytes 3760132
  524.3 51.9 %copy-start.10 = (pred[17,144,128]{2,1,0:T(8,128)(4,1)S(1)}, pred[17,144,128]{2,1,0:T(8,128)(4,1)}, u32[]{:S(2)}) copy-start(pred[17,144,128]{2,1,0:T(8,128)(4,1)} %copy-done.9) | copy-start | bytes 940036
  524.3 51.9 %copy-start.14 = (f32[4]{0:T(128)S(1)}, f32[4]{0:T(128)}, u32[]{:S(2)}) copy-start(f32[4]{0:T(128)} %copy-done.13) | copy-start | bytes 52
  524.3 51.9 %copy-start.16 = (f32[4]{0:T(128)S(1)}, f32[4]{0:T(128)}, u32[]{:S(2)}) copy-start(f32[4]{0:T(128)} %copy-done.15) | copy-start | bytes 52
  524.3 51.9 %copy-start.18 = (f32[4]{0:T(128)S(1)}, f32[4]{0:T(128)}, u32[]{:S(2)}) copy-start(f32[4]{0:T(128)} %copy-done.17) | copy-start | bytes 52
  524.3 51.9 %copy-start.20 = (f32[4]{0:T(128)S(1)}, f32[4]{0:T(128)}, u32[]{:S(2)}) copy-start(f32[4]{0:T(128)} %copy-done.19) | copy-start | bytes 52
  524.3 51.9 %copy-start.22 = (f32[4]{0:T(128)S(1)}, f32[4]{0:T(128)}, u32[]{:S(2)}) copy-start(f32[4]{0:T(128)} %copy-done.21) | copy-start | bytes 52
  524.3 51.9 %copy-start.24 = (f32[17]{0:T(128)S(1)}, f32[17]{0:T(128)}, u32[]{:S(2)}) copy-start(f32[17]{0:T(128)} %copy-done.23) | copy-start | bytes 208
  625.5 48.7 %collective-permute-start.4 = (f32[2048,256]{1,0:T(8,128)}, f32[2048,256]{1,0:T(8,128)}, u32[]{:S(2)}, u32[]{:S(2)}) collective-permute-start(f32[2048,256]{1,0:T(8,128)} %copy.167), channel_id=1, source_target_pairs={{0,1},{1,0},{2,3},{3,2},{4,5},{5,4},{6,7},{7,6},{8,9},{9,8},{10,11... | collective-permute-start | bytes 6291464 | tf_op jit(solution)/shard_map/ppermute | solution.py:33
  627.0 51.0 %copy-start.1 = (f32[16,128,128]{2,1,0:T(8,128)S(1)}, f32[16,128,128]{2,1,0:T(8,128)}, u32[]{:S(2)}) copy-start(f32[16,128,128]{2,1,0:T(8,128)} %param.6) | copy-start | bytes 3145732
  (1 other events, 0.7 us)
